TPU v7x, 512 devices: a whole 4x4x16 slice. The times are simulated.
512 devices in a mesh: dp: 8 (over y, core), tensor: 64 (over z, x).
Axes of the slice: x: 4, y: 4, z: 16, core: 2. Of those that a mesh axis runs over, the one named last changes fastest.
Arguments:
- hidden_states: bfloat16 [8192, 2560], P(('dp', 'tensor')), may hold values from -8 to 8
- norm_gain: float32 [2560], replicated, may hold values from 0.5 to 1.5
- head_weight: bfloat16 [2560, 76032], P('dp', 'tensor'), may hold values from -8 to 8
- targets: int32 [8192], P(('dp', 'tensor')), may hold values from 0 to 76031
- lengths: int32 [8, 16], P('dp'), may hold values from 1 to 512, 1024 in all within a row
Outputs:
- log_prob: float32 [8192], P(('dp', 'tensor'))
- entropy: float32 [8192], P(('dp', 'tensor'))
- seq_mean: float32 [8, 16], P('dp')
Inputs may be any that keep to these rules, and one draw needn't show every extreme that they name: Each data group's lengths sum to 16 * 64.
All inputs are finite; a program needn't handle non-finite values.
Results may differ from a plain program's by a relative error of at most 0.0072.
Values may be sent and summed in bfloat16 or wider, within the bound.
A program may use at most 64 MiB of HBM per device.

v0:
```python
import jax
import jax.numpy as jnp
from jax import lax
from jax.sharding import PartitionSpec as P


def shard_stats(logits, wanted, vocab_start):
    highest = jnp.max(logits, axis=1)
    expo = jnp.exp(logits - highest[:, None])
    totals = jnp.sum(expo, axis=1)
    weighted = jnp.sum(expo * logits, axis=1)
    columns = lax.broadcasted_iota(jnp.int32, logits.shape, 1)
    picked = jnp.sum(jnp.where(columns == (wanted - vocab_start)[:, None], logits, 0.0), axis=1)
    return jnp.stack([highest, totals, weighted, picked])


def by_blocks(work, matrix_rows, wanted):
    row_count = matrix_rows.shape[0]
    block_count = row_count // 512

    def one_block(couple):
        return work(couple[0], couple[1])

    results = lax.map(
        one_block,
        (
            matrix_rows.reshape(block_count, 512, matrix_rows.shape[1]),
            wanted.reshape(block_count, 512),
        ),
    )
    return jnp.transpose(results, (1, 0, 2)).reshape(4, row_count)


def finish_rows(largest, sum_exp, sum_weighted, sum_picked):
    lse = largest + jnp.log(sum_exp)
    return (sum_picked - lse, lse - sum_weighted / sum_exp)


def sequence_sums(values, seq_lengths, seq_count):
    positions = jnp.arange(values.shape[0], dtype=jnp.int32)
    seq_ends = jnp.cumsum(seq_lengths)
    segment = jnp.sum((positions[:, None] >= seq_ends[None, :]).astype(jnp.int32), axis=1)
    onehot = segment[:, None] == jnp.arange(seq_count, dtype=jnp.int32)[None, :]
    return jnp.sum(jnp.where(onehot, values[:, None], 0.0), axis=0)


def on_device(hidden_states, norm_gain, head_weight, targets, lengths):
    widths = hidden_states.astype(jnp.float32)
    meansq = jnp.mean(widths * widths, axis=1, keepdims=True)
    normed = (widths * lax.rsqrt(meansq + 1e-06) * norm_gain).astype(jnp.bfloat16)
    vocab_part = head_weight.shape[1]
    tensor_index = lax.axis_index("tensor")
    vocab_start = tensor_index * vocab_part
    own_rows = hidden_states.shape[0]
    own_start = tensor_index * own_rows
    seq_lengths = lengths[0]
    seq_count = lengths.shape[1]
    wanted_all = lax.all_gather(targets, "tensor", axis=0, tiled=True)
    rows_all = lax.all_gather(normed, "tensor", axis=0, tiled=True)
    logits = jnp.dot(
        rows_all,
        lax.all_gather(head_weight, "dp", axis=0, tiled=True),
        preferred_element_type=jnp.float32,
    )

    def logit_stats(block_logits, block_wanted):
        return shard_stats(block_logits, block_wanted, vocab_start)

    row_table = by_blocks(logit_stats, logits, wanted_all)
    highest = row_table[0]
    totals = row_table[1]
    weighted = row_table[2]
    picked = row_table[3]
    largest = lax.pmax(highest, "tensor")
    factor = jnp.exp(highest - largest)
    sum_exp, sum_weighted, sum_picked = lax.psum(
        (totals * factor, weighted * factor, picked), "tensor"
    )
    group_logprob, group_entropy = finish_rows(largest, sum_exp, sum_weighted, sum_picked)
    sums = sequence_sums(group_logprob, seq_lengths, seq_count)
    log_prob = lax.dynamic_slice_in_dim(group_logprob, own_start, own_rows, 0)
    entropy = lax.dynamic_slice_in_dim(group_entropy, own_start, own_rows, 0)
    seq_mean = (sums / seq_lengths.astype(jnp.float32))[None, :]
    return (log_prob, entropy, seq_mean)


def solution(mesh):
    in_specs = (
        P(("dp", "tensor"), None),
        P(),
        P("dp", "tensor"),
        P(("dp", "tensor")),
        P("dp", None),
    )
    out_specs = (P(("dp", "tensor")), P(("dp", "tensor")), P("dp", None))
    return jax.shard_map(
        on_device, mesh=mesh, in_specs=in_specs, out_specs=out_specs, check_vma=False
    )
```

profile of v0, /device:TPU:24, one launch (start us, length us, event | category | flops | bytes accessed | tf_op | source)
XLA Modules:
  0.0 657.5 jit_solution(5995464024630584219)
XLA Ops:
  7.2 0.0 all-gather.3.cloned.1.call-start
  7.2 1.0 fusion.5
  8.2 1.6 fusion.7
  9.8 0.0 all-gather.3.cloned.1.call-update
  9.9 0.0 all-gather.5.cloned.1.call-start
  9.9 0.7 all-gather.5.cloned.1.call-update
  10.6 1.3 dynamic-slice
  12.6 0.9 dynamic-update-slice
  13.4 34.0 %all-reduce = s32[1024]{0:T(1024)S(1)} all-reduce(s32[1024]{0:T(1024)S(1)} %dynamic-update-slice), channel_id=1, replica_groups=mesh['dp'=8,'tensor'=64] {'tensor'}, use_global_device_ids=true, to_apply=%add | all-reduce | flops 1024 | bytes 8192
  47.5 0.7 copy.13
  48.2 0.1 reduce.1
  48.4 0.1 convert_reduce_fusion
  48.4 116.6 %all-gather.3.cloned.1.call-done = bf16[1024,2560]{1,0:T(8,128)(2,1)} async-done(((bf16[16,2560]{1,0:T(8,128)(2,1)}), bf16[1024,2560]{1,0:T(8,128)(2,1)}) %all-gather.3.cloned.1.call-update) | async-done | bytes 5242896 | tf_op jit(solution)/shard_map/all_gather | solution.py:59
  165.1 44.0 %all-gather.5.cloned.1.call-done = bf16[2560,1188]{1,0:T(8,128)(2,1)} async-done(((bf16[320,1188]{1,0:T(8,128)(2,1)}), bf16[2560,1188]{1,0:T(8,128)(2,1)}) %all-gather.5.cloned.1.call-update) | async-done | bytes 6082576 | tf_op jit(solution)/shard_map/all_gather | solution.py:62
  209.0 12.2 %fusion.12 = f32[1024,1188]{1,0:T(8,128)} fusion(bf16[1024,2560]{1,0:T(8,128)(2,1)} %all-gather.3.cloned.1.call-done, bf16[2560,1188]{1,0:T(8,128)(2,1)} %all-gather.5.cloned.1.call-done), kind=kOutput, calls=%fused_computation.30 | convolution fusion | flops 6228541440 | bytes 16191488 | tf_op jit(solution)/shard_map/while | solution.py:24
  221.2 0.0 copy-start
  221.2 9.5 %while.10 = (s32[]{:T(128)}, f32[2,4,512]{2,1,0:T(4,128)S(1)}, f32[2,512,1188]{2,1,0:T(8,128)}, s32[2,512]{1,0:T(2,128)S(1)}, s32[]{:T(128)}, /*index=5*/s32[]{:T(128)}) while((s32[]{:T(128)}, f32[2,4,512]{2,1,0:T(4,128)S(1)}, f32[2,512,1188]{2,1,0:T(8,128)}, s32[2,512]{1,0:T(2,128)S(1)}, s32[]{:T(128)}, /*index=5*/s32[]{:T(128)}) %tuple.41), condition=%wide.region_6.7_spmd, body=%wide.region_1.6_spmd.sunk | while | flops 4870658 | bytes 4898905 | solution.py:24
  221.2 1.9 dynamic-slice_reduce_fusion.2
  223.2 2.7 fusion.17
  226.0 1.9 dynamic-slice_reduce_fusion.2
  227.9 2.7 fusion.17
  230.7 144.2 %pmax.7 = f32[1024]{0:T(1024)S(1)} all-reduce(f32[1024]{0:T(1024)S(1)} %bitcast.55), channel_id=1, replica_groups=mesh['dp'=8,'tensor'=64] {'tensor'}, use_global_device_ids=true, to_apply=%region_8.9 | all-reduce | flops 1024 | bytes 8192 | tf_op jit(solution)/shard_map/pmax | solution.py:74
  374.9 274.0 %all-reduce.1 = (f32[1024]{0:T(1024)S(1)}, f32[1024]{0:T(1024)S(1)}, f32[1024]{0:T(1024)S(1)}) all-reduce(f32[1024]{0:T(1024)S(1)} %bitcast.58, f32[1024]{0:T(1024)S(1)} %get-tuple-element.69, f32[1024]{0:T(1024)S(1)} %get-tuple-element.68), channel_id=1, replica_groups=mesh['dp'=8,'tensor'=64] {'tensor'}, use_global_device_ids=true, to_apply=%region_7.8 | all-reduce | flops 3072 | bytes 24576 | tf_op jit(solution)/shard_map/psum | solution.py:76
  648.9 0.1 select_reduce_fusion
  649.0 0.0 copy-done
  649.0 0.5 bitcast_divide_fusion
  649.5 0.6 dynamic_slice.14
  650.1 0.6 dynamic_slice.15
  (12 shorter events, 0.2 us)
Async XLA Ops:
  7.2 157.9 %all-gather.3.cloned.1.call-start = ((), (), s32[]{:S(2)}) async-start(), calls=%async_computation | async-start | bytes 5324800 | tf_op jit(solution)/shard_map/all_gather | solution.py:59
  9.9 199.2 %all-gather.5.cloned.1.call-start = ((), (), s32[]{:S(2)}) async-start(), calls=%async_computation.1 | async-start | bytes 7372800 | tf_op jit(solution)/shard_map/all_gather | solution.py:62
  221.2 427.8 %copy-start = (s32[1,16]{1,0:T(1,128)S(1)}, s32[1,16]{1,0:T(1,128)}, u32[]{:S(2)}) copy-start(s32[1,16]{1,0:T(1,128)} %param.11) | copy-start | bytes 196
Sparse Core Ops, SparseCore 0:
  10.9 154.0 all-gather.2
  167.2 41.8 all-gather.4
where the time goes:
time: 659 us; the launch traced here: 658 us
  blocking collectives  452 us (69%)
  waiting for transfers between devices  161 us (24%)
  between operations  14.7 us (2%)
  other arithmetic  13 us (2%)
  matrix products  12.2 us (2%)
    psum x1, blocking collectives, on_device(): lax.psum((totals * factor, weighted * factor, picked), 'tensor')  274 us
    pmax x1, blocking collectives, on_device(): largest = lax.pmax(highest, 'tensor')  144 us
    all_gather x1, waiting for transfers between devices, on_device(): rows_all = lax.all_gather(normed, 'tensor', axis=0, tiled=True)  117 us
    all_gather x1, waiting for transfers between devices, on_device(): lax.all_gather(head_weight, 'dp', axis=0, tiled=True)  44 us
    unnamed x1, blocking collectives  34 us
  transfers between devices with their start and end apart: 2, of which 2 were waited for; matrix products, arithmetic and copies ran while one was open for 0% of the time, Pallas kernels for 0%

commit v1 on v0

v1 whole, which is shorter than its diff:
```python
import functools

import jax
import jax.numpy as jnp
from jax import lax
from jax.experimental import pallas as pl
from jax.experimental.pallas import tpu as pltpu
from jax.sharding import PartitionSpec as P

MESH = pl.DeviceIdType.MESH
NX = 4
NY = 4
LANES = 128
CHUNKS = 4
EVENTS = 6


def split_columns(width):
    tiles = width // LANES
    first = max(1, round(tiles * 0.4)) * LANES
    rest = (width - first) // LANES + 1
    return first, first + rest // 2 * LANES


def kernel(nz, hidden_ref, gain_ref, w_hbm, targets_ref, lens_ref, lensv_ref,
           logp_ref, ent_ref, mean_ref,
           rows, wts, logits, stats, ex, sz_own, sz_a, sx_a, sx1, sx2, sw, sc, sex, ssend, sload):
    own_rows, width = hidden_ref.shape
    vocab = w_hbm.shape[-1]
    half = nz // 2
    ca, cm = split_columns(width)
    wide = width + LANES

    t = lax.axis_index("tensor")
    d = lax.axis_index("dp")
    z, x = t // NX, t % NX
    y, c = d // 2, d % 2
    zg = nz // 4

    def tensor_at(zz, xx):
        return {"tensor": zz * NX + xx}

    def dp_at(yy, cc):
        return {"dp": yy * 2 + cc}

    right, left = lax.rem(x + 1, NX), lax.rem(x + NX - 1, NX)
    across = lax.rem(x + 2, NX)
    up, down = lax.rem(z + 1, nz), lax.rem(z + nz - 1, nz)
    north, south = lax.rem(y + 1, NY), lax.rem(y + NY - 1, NY)

    load = pltpu.make_async_copy(w_hbm, wts.at[d], sload)
    load.start()

    barrier = pltpu.get_barrier_semaphore()
    peers = [tensor_at(z, right), tensor_at(z, left), tensor_at(z, across),
             tensor_at(up, x), tensor_at(down, x),
             dp_at(north, c), dp_at(south, c), dp_at(y, 1 - c)]
    peers += [tensor_at(z // 4 * 4 + lax.rem(z + i, 4), x) for i in (1, 2, 3)]
    peers += [tensor_at(lax.rem(z // 4 + i, zg) * 4 + z % 4, x) for i in range(1, zg)]
    for peer in peers:
        pl.semaphore_signal(barrier, inc=1, device_id=peer, device_id_type=MESH)

    widths = hidden_ref[...].astype(jnp.float32)
    meansq = jnp.sum(widths * widths, axis=1, keepdims=True) / width
    normed = widths * lax.rsqrt(meansq + 1e-06) * gain_ref[...]
    rows[z, x, :, 0:width] = normed.astype(jnp.bfloat16)
    row_id = lax.broadcasted_iota(jnp.int32, (own_rows, LANES), 0)
    lane = lax.broadcasted_iota(jnp.int32, (own_rows, LANES), 1)
    ids = jnp.zeros((own_rows, LANES), jnp.int32)
    for i in range(own_rows):
        ids = jnp.where(row_id == i, targets_ref[i], ids)
    digits = jnp.where(lane == 0, ids >> 16, jnp.where(lane == 1, (ids >> 8) & 255, ids & 255))
    digits = jnp.where(lane < 3, digits, 0)
    rows[z, x, :, width:wide] = digits.astype(jnp.float32).astype(jnp.bfloat16)

    pl.semaphore_wait(barrier, len(peers))

    def push(ref, send, recv, peer):
        pltpu.make_async_remote_copy(
            src_ref=ref, dst_ref=ref, send_sem=send, recv_sem=recv,
            device_id=peer, device_id_type=MESH,
        ).start()

    def got(ref, sem):
        pltpu.make_async_copy(ref, ref, sem).wait()

    def send_own(zo, to, way, step):
        push(rows.at[zo, x], ssend.at[0], sz_own.at[way, step], tensor_at(to, x))

    def send_a(zo, to, way, step):
        for i in (1, 2, 3):
            xo = lax.rem(x + i, NX)
            push(rows.at[zo, xo, :, pl.ds(0, ca)], ssend.at[1], sz_a.at[way, step], tensor_at(to, x))

    three_a = rows.at[0, pl.ds(0, 3), :, pl.ds(0, ca)]

    def send_x(zo):
        block = rows.at[zo, x, :, pl.ds(ca, wide - ca)]
        push(block, ssend.at[3], sx1.at[0, zo], tensor_at(z, right))
        push(block, ssend.at[3], sx1.at[1, zo], tensor_at(z, left))

    def forward_x(zo):
        got(rows.at[zo, left, :, pl.ds(ca, wide - ca)], sx1.at[0, zo])
        push(rows.at[zo, left, :, pl.ds(ca, cm - ca)], ssend.at[4], sx2.at[0, zo], tensor_at(z, right))
        got(rows.at[zo, right, :, pl.ds(ca, wide - ca)], sx1.at[1, zo])
        push(rows.at[zo, right, :, pl.ds(cm, wide - cm)], ssend.at[5], sx2.at[1, zo], tensor_at(z, left))

    def weight_event(j):
        for way in (0, 1):
            hop = 1 + j // CHUNKS
            yo = lax.rem(y + (NY - hop if way == 0 else hop), NY)
            piece = lax.rem(j + 2 * way, CHUNKS)
            ref = wts.at[yo * 2 + c, piece]
            got(ref, sw.at[way, j])

            @pl.when(j < 2)
            def _():
                push(ref, ssend.at[6], sw.at[way, j + CHUNKS], dp_at(north if way == 0 else south, c))

            push(ref, ssend.at[7], sc.at[way, j], dp_at(y, 1 - c))

    send_own(z, up, 0, 1)
    send_own(z, down, 1, 1)
    for i, (xo, slot) in enumerate(((right, 0), (left, 1), (across, 2))):
        push(rows.at[z, x, :, pl.ds(0, ca)], ssend.at[2], sx_a.at[slot], tensor_at(z, xo))
    send_x(z)
    load.wait()
    for j in range(CHUNKS):
        push(wts.at[d, j], ssend.at[6], sw.at[0, j], dp_at(north, c))
        piece = (j + 2) % CHUNKS
        push(wts.at[d, piece], ssend.at[6], sw.at[1, j], dp_at(south, c))
    for j in range(CHUNKS):
        push(wts.at[d, j], ssend.at[7], sc.at[2, j], dp_at(y, 1 - c))
    got(rows.at[z, left, :, pl.ds(0, ca)], sx_a.at[0])
    got(rows.at[z, right, :, pl.ds(0, ca)], sx_a.at[1])
    got(rows.at[z, across, :, pl.ds(0, ca)], sx_a.at[2])
    send_a(z, up, 0, 1)
    send_a(z, down, 1, 1)

    def ring_step(k, _):
        below, above = lax.rem(z + nz - k, nz), lax.rem(z + k, nz)
        got(rows.at[below, x], sz_own.at[0, k])
        send_own(below, up, 0, k + 1)
        got(rows.at[above, x], sz_own.at[1, k])

        @pl.when(k < half - 1)
        def _():
            send_own(above, down, 1, k + 1)

        send_x(below)
        send_x(above)
        got(three_a, sz_a.at[0, k])

        @pl.when(k < half - 1)
        def _():
            send_a(below, up, 0, k + 1)

        got(three_a, sz_a.at[1, k])
        send_a(above, down, 1, k + 1)

        forward_x(lax.rem(z + nz - k + 1, nz))

        @pl.when(k > 1)
        def _():
            forward_x(lax.rem(z + k - 1, nz))

        @pl.when(k <= EVENTS)
        def _():
            weight_event(k - 1)

        return 0

    lax.fori_loop(1, half, ring_step, 0)
    far = lax.rem(z + half, nz)
    got(rows.at[far, x], sz_own.at[0, half])
    send_x(far)
    if half > 1:
        forward_x(lax.rem(z + half + 1, nz))
    if half > 2:
        forward_x(lax.rem(z + half - 1, nz))
    for j in range(half - 1, EVENTS):
        weight_event(jnp.int32(j))
    got(three_a, sz_a.at[1, half])
    forward_x(far)

    def last_x(zo, _):
        got(rows.at[zo, across, :, pl.ds(ca, cm - ca)], sx2.at[0, zo])
        got(rows.at[zo, across, :, pl.ds(cm, wide - cm)], sx2.at[1, zo])
        return 0

    lax.fori_loop(0, nz, last_x, 0)

    def last_w(j, _):
        got(wts.at[0, 0], sc.at[0, j])
        got(wts.at[0, 0], sc.at[1, j])
        return 0

    lax.fori_loop(0, EVENTS, last_w, 0)
    for j in range(CHUNKS):
        got(wts.at[0, 0], sc.at[2, j])

    zs = 256 // (NX * own_rows)
    block = 256
    vocab_start = t * vocab
    lane_w = lax.broadcasted_iota(jnp.int32, (1, LANES), 1)
    digit_weights = jnp.where(lane_w == 0, 65536.0, jnp.where(lane_w == 1, 256.0, jnp.where(lane_w == 2, 1.0, 0.0)))

    def score(b, _):
        held = rows.at[pl.ds(b * zs, zs)]
        lhs = held[:, :, :, 0:width].reshape(block, width)
        rhs = wts[...].reshape(width, vocab)
        logits[...] = jnp.dot(lhs, rhs, preferred_element_type=jnp.float32)
        coded = held[:, :, :, width:wide].reshape(block, LANES).astype(jnp.float32)
        wanted = jnp.sum(coded * digit_weights, axis=1, keepdims=True).astype(jnp.int32) - vocab_start
        values = logits[...]
        highest = jnp.max(values, axis=1, keepdims=True)
        expo = jnp.exp(values - highest)
        total = jnp.sum(expo, axis=1, keepdims=True)
        weighted = jnp.sum(expo * values, axis=1, keepdims=True)
        columns = lax.broadcasted_iota(jnp.int32, values.shape, 1)
        picked = jnp.sum(jnp.where(columns == wanted, values, 0.0), axis=1, keepdims=True)
        at = lax.broadcasted_iota(jnp.int32, (block, LANES), 1)
        table = jnp.where(at == 0, highest, jnp.where(at == 1, total, jnp.where(at == 2, weighted, picked)))
        flat = jnp.transpose(table)
        for s in range(4):
            for q in range(block // LANES):
                stats[s, pl.ds(b * (block // LANES) + q, 1), :] = flat[s:s + 1, q * LANES:(q + 1) * LANES]
        return 0

    lax.fori_loop(0, nz // zs, score, 0)

    def exchange(stage, mine, size, peer_of):
        ex[stage, mine] = stats[...]
        for i in range(1, size):
            push(ex.at[stage, mine], ssend.at[8], sex.at[stage], peer_of(lax.rem(mine + i, size)))
        if size > 1:
            got(ex.at[stage, pl.ds(0, size - 1)], sex.at[stage])
        top = ex[stage, 0, 0]
        for i in range(1, size):
            top = jnp.maximum(top, ex[stage, i, 0])
        sums = [jnp.zeros_like(top) for _ in range(3)]
        for i in range(size):
            factor = jnp.exp(ex[stage, i, 0] - top)
            sums[0] += ex[stage, i, 1] * factor
            sums[1] += ex[stage, i, 2] * factor
            sums[2] += ex[stage, i, 3]
        stats[0] = top
        for i in range(3):
            stats[i + 1] = sums[i]

    exchange(0, x, NX, lambda i: tensor_at(z, i))
    exchange(1, z % 4, 4, lambda i: tensor_at(z // 4 * 4 + i, x))
    exchange(2, z // 4, zg, lambda i: tensor_at(i * 4 + z % 4, x))

    lse = stats[0] + jnp.log(stats[1])
    group_logp = stats[3] - lse
    group_ent = lse - stats[2] / stats[1]
    shape = group_logp.shape
    stats[0] = group_logp
    stats[1] = group_ent
    per = LANES // own_rows
    turn = lax.rem(LANES - t % per * own_rows, LANES)
    for ref, s in ((logp_ref, 0), (ent_ref, 1)):
        line = stats[s, pl.ds(t // per, 1), :]
        ref[...] = pltpu.roll(jnp.broadcast_to(line, (8, LANES)), turn, 1)[0:1, 0:own_rows]

    position = lax.broadcasted_iota(jnp.int32, shape, 0) * LANES + lax.broadcasted_iota(jnp.int32, shape, 1)
    count = lens_ref.shape[1]
    slot = lax.broadcasted_iota(jnp.int32, (1, count), 1)
    sums = jnp.zeros((1, count), jnp.float32)
    start = jnp.int32(0)
    for q in range(count):
        end = start + lens_ref[0, q]
        inside = (position >= start) & (position < end)
        part = jnp.sum(jnp.sum(jnp.where(inside, group_logp, 0.0), axis=0, keepdims=True), axis=1, keepdims=True)
        sums = jnp.where(slot == q, part, sums)
        start = end
    mean_ref[...] = sums / lensv_ref[...].astype(jnp.float32)

    got(rows.at[pl.ds(0, nz - 1), 0], ssend.at[0])
    got(rows.at[pl.ds(0, nz - 1), pl.ds(0, 3), :, pl.ds(0, ca)], ssend.at[1])
    got(three_a, ssend.at[2])
    got(rows.at[:, pl.ds(0, 2), :, pl.ds(ca, wide - ca)], ssend.at[3])
    got(rows.at[:, 0, :, pl.ds(ca, cm - ca)], ssend.at[4])
    got(rows.at[:, 0, :, pl.ds(cm, wide - cm)], ssend.at[5])
    got(wts.at[pl.ds(0, 3)], ssend.at[6])
    got(wts.at[pl.ds(0, 4)], ssend.at[7])
    for stage, size in ((0, NX), (1, 4), (2, zg)):
        if size > 1:
            got(ex.at[stage, pl.ds(0, size - 1)], ssend.at[8])


def on_device(nz, hidden_states, norm_gain, head_weight, targets, lengths):
    own_rows, width = hidden_states.shape
    depth, vocab = head_weight.shape
    wide = width + LANES
    group_rows = nz * NX * own_rows
    vmem = pl.BlockSpec(memory_space=pltpu.VMEM)
    smem = pl.BlockSpec(memory_space=pltpu.SMEM)
    dma = pltpu.SemaphoreType.DMA
    logp, ent, mean = pl.pallas_call(
        functools.partial(kernel, nz),
        out_shape=(
            jax.ShapeDtypeStruct((1, own_rows), jnp.float32),
            jax.ShapeDtypeStruct((1, own_rows), jnp.float32),
            jax.ShapeDtypeStruct(lengths.shape, jnp.float32),
        ),
        in_specs=[vmem, vmem, pl.BlockSpec(memory_space=pl.ANY), smem, smem, vmem],
        out_specs=(vmem, vmem, vmem),
        scratch_shapes=[
            pltpu.VMEM((nz, NX, own_rows, wide), jnp.bfloat16),
            pltpu.VMEM((2 * NY, CHUNKS, depth // CHUNKS, vocab), jnp.bfloat16),
            pltpu.VMEM((256, vocab), jnp.float32),
            pltpu.VMEM((4, group_rows // LANES, LANES), jnp.float32),
            pltpu.VMEM((3, 4, 4, group_rows // LANES, LANES), jnp.float32),
            dma((2, nz // 2 + 1)),
            dma((2, nz // 2 + 1)),
            dma((3,)),
            dma((2, nz)),
            dma((2, nz)),
            dma((2, EVENTS)),
            dma((3, EVENTS)),
            dma((3,)),
            dma((9,)),
            dma,
        ],
        compiler_params=pltpu.CompilerParams(
            collective_id=0, has_side_effects=True, vmem_limit_bytes=48 << 20
        ),
    )(hidden_states, norm_gain[None, :], head_weight.reshape(CHUNKS, depth // CHUNKS, vocab),
      targets, lengths, lengths)
    return logp[0], ent[0], mean


def solution(mesh):
    in_specs = (
        P(("dp", "tensor"), None),
        P(),
        P("dp", "tensor"),
        P(("dp", "tensor")),
        P("dp", None),
    )
    out_specs = (P(("dp", "tensor")), P(("dp", "tensor")), P("dp", None))
    return jax.shard_map(
        functools.partial(on_device, mesh.shape["tensor"] // NX),
        mesh=mesh, in_specs=in_specs, out_specs=out_specs, check_vma=False,
    )
```

time: 659 us -> 89.3 us (0.14)
  blocking collectives: 452 us -> 0 us
  waiting for transfers between devices: 161 us -> 0 us
  Pallas kernels: 0 us -> 83.9 us
  between operations: 14.7 us -> 0.68 us
  other arithmetic: 13 us -> 0 us
  matrix products: 12.2 us -> 0 us
    psum x1 -> x0, blocking collectives: 274 us -> none  [on_device(): lax.psum((totals * factor, weighted * factor, picked), 'tensor')]
    all_gather x2 -> x0, waiting for transfers between devices: 161 us -> none  [the longest x1 117 us: on_device(): rows_all = lax.all_gather(normed, 'tensor', axis=0, tiled=True)]
    pmax x1 -> x0, blocking collectives: 144 us -> none  [on_device(): largest = lax.pmax(highest, 'tensor')]
    pallas_call x0 -> x1, Pallas kernels: none -> 83.9 us  [on_device(): pl.pallas_call(functools.partial(kernel, nz), out_shape=(jax.ShapeDtypeSt...]
    unnamed x1 -> x0, blocking collectives: 34 us -> none
    while x1 -> x0, matrix products: 12.2 us -> none  [by_blocks(): lax.map(one_block, (matrix_rows.reshape(block_count, 512, matrix_rows.sha...]
    reduce_sum x5 -> x0, other arithmetic: 6.71 us -> none  [the longest x2 5.48 us: shard_stats(): totals = jnp.sum(expo, axis=1)]
  transfers between devices with their start and end apart: 2 -> 0, of which waited for: 2 -> 0; matrix products, arithmetic and copies ran while one was open for 0% -> 0% of each run, Pallas kernels for 0% -> 0%
where the time goes in v1:
time: 89.3 us; the launch traced here: 88.8 us
  Pallas kernels  83.9 us (94%)
  local copies, waits for them, and re-layouts  4.3 us (5%)
    pallas_call x1, Pallas kernels, on_device(): pl.pallas_call(functools.partial(kernel, nz), out_shape=(jax.ShapeDtypeSt...  83.9 us
    unnamed x11, local copies, waits for them, and re-layouts  3.57 us

profile of v1, /device:TPU:24, one launch (start us, length us, event | category | flops | bytes accessed | tf_op | source)
XLA Modules:
  0.0 88.8 jit_solution(5072523725003831310)
XLA Ops:
  0.6 0.0 copy-start.2
  0.6 0.0 copy-start.3
  0.7 0.7 broadcast_in_dim.3.gain_ref
  1.4 0.0 copy-done.2
  1.4 0.0 copy-done.3
  1.4 0.0 copy-start
  1.4 1.1 %copy-done = bf16[320,1188]{1,0:T(8,128)(2,1)S(1)} copy-done((bf16[320,1188]{1,0:T(8,128)(2,1)S(1)}, bf16[320,1188]{1,0:T(8,128)(2,1)}, u32[]{:S(2)}) %copy-start) | copy-done | bytes 760344
  2.5 0.0 copy-start.1
  2.5 0.9 copy-done.1
  3.4 83.9 %shard_map.76 = (f32[1,16]{1,0:T(1,128)S(1)}, f32[1,16]{1,0:T(1,128)S(1)}, f32[1,16]{1,0:T(1,128)S(1)}) custom-call(bf16[16,2560]{1,0:T(8,128)(2,1)S(1)} %copy-done.1, f32[1,2560]{1,0:T(1,128)S(1)} %broadcast_in_dim.3.gain_ref, bf16[4,80,1188]{2,1,0:T(8,128)(2,1)S(1)} %bitcast.3, s32[16]{0:T(128)S(1)} %copy-done.3, s32[1,16]{1,0:T(1,128)S(1)} %copy-done.2, ...), custom_call_target="tpu_custom_call" | custom-call | tf_op jit(solution)/shard_map/pallas_call | solution.py:301
  87.3 0.5 copy.11
  87.8 0.5 copy.12
  88.3 0.5 copy.13
Async XLA Ops:
  0.6 0.7 copy-start.2
  0.6 0.7 copy-start.3
  1.4 1.1 %copy-start = (bf16[320,1188]{1,0:T(8,128)(2,1)S(1)}, bf16[320,1188]{1,0:T(8,128)(2,1)}, u32[]{:S(2)}) copy-start(bf16[320,1188]{1,0:T(8,128)(2,1)} %param.7) | copy-start | bytes 2280964
  2.5 0.9 copy-start.1

commit v2 on v1

--- a/solution.py
+++ b/solution.py
@@ -22,9 +22,10 @@
     return first, first + rest // 2 * LANES
 
 
-def kernel(nz, hidden_ref, gain_ref, w_hbm, targets_ref, lens_ref, lensv_ref,
-           logp_ref, ent_ref, mean_ref,
-           rows, wts, logits, stats, ex, sz_own, sz_a, sx_a, sx1, sx2, sw, sc, sex, ssend, sload):
+def kernel(nz, hidden_hbm, gain_hbm, w_hbm, targets_hbm, lens_hbm,
+           out_ref,
+           hidden_ref, gain_ref, targets_ref, lens_ref,
+           rows, wts, logits, stats, ex, sz_b, sz_a, sx_a, sx1, sx2, sw, sc, sex, ssend, sload):
     own_rows, width = hidden_ref.shape
     vocab = w_hbm.shape[-1]
     half = nz // 2
@@ -48,22 +49,30 @@
     up, down = lax.rem(z + 1, nz), lax.rem(z + nz - 1, nz)
     north, south = lax.rem(y + 1, NY), lax.rem(y + NY - 1, NY)
 
-    load = pltpu.make_async_copy(w_hbm, wts.at[d], sload)
-    load.start()
+    loads = [
+        pltpu.make_async_copy(src, dst, sload.at[i])
+        for i, (src, dst) in enumerate((
+            (hidden_hbm, hidden_ref), (gain_hbm, gain_ref), (targets_hbm, targets_ref),
+            (lens_hbm, lens_ref), (w_hbm, wts.at[d])))
+    ]
+    for load in loads:
+        load.start()
 
     barrier = pltpu.get_barrier_semaphore()
     peers = [tensor_at(z, right), tensor_at(z, left), tensor_at(z, across),
              tensor_at(up, x), tensor_at(down, x),
              dp_at(north, c), dp_at(south, c), dp_at(y, 1 - c)]
-    peers += [tensor_at(z // 4 * 4 + lax.rem(z + i, 4), x) for i in (1, 2, 3)]
-    peers += [tensor_at(lax.rem(z // 4 + i, zg) * 4 + z % 4, x) for i in range(1, zg)]
     for peer in peers:
         pl.semaphore_signal(barrier, inc=1, device_id=peer, device_id_type=MESH)
 
+    for load in loads[:4]:
+        load.wait()
     widths = hidden_ref[...].astype(jnp.float32)
     meansq = jnp.sum(widths * widths, axis=1, keepdims=True) / width
-    normed = widths * lax.rsqrt(meansq + 1e-06) * gain_ref[...]
-    rows[z, x, :, 0:width] = normed.astype(jnp.bfloat16)
+    scaled = widths * lax.rsqrt(meansq + 1e-06)
+    for i in range(width // LANES):
+        cols = slice(i * LANES, (i + 1) * LANES)
+        rows[z, x, :, cols] = (scaled[:, cols] * gain_ref[i:i + 1, :]).astype(jnp.bfloat16)
     row_id = lax.broadcasted_iota(jnp.int32, (own_rows, LANES), 0)
     lane = lax.broadcasted_iota(jnp.int32, (own_rows, LANES), 1)
     ids = jnp.zeros((own_rows, LANES), jnp.int32)
@@ -84,15 +93,19 @@
     def got(ref, sem):
         pltpu.make_async_copy(ref, ref, sem).wait()
 
-    def send_own(zo, to, way, step):
-        push(rows.at[zo, x], ssend.at[0], sz_own.at[way, step], tensor_at(to, x))
-
-    def send_a(zo, to, way, step):
-        for i in (1, 2, 3):
-            xo = lax.rem(x + i, NX)
-            push(rows.at[zo, xo, :, pl.ds(0, ca)], ssend.at[1], sz_a.at[way, step], tensor_at(to, x))
-
-    three_a = rows.at[0, pl.ds(0, 3), :, pl.ds(0, ca)]
+    b_cols = (pl.ds(ca, cm - ca), pl.ds(cm, wide - cm))
+
+    def b_piece(zo, i):
+        return rows.at[zo, x, :, b_cols[i]]
+
+    def a_piece(zo, i):
+        return rows.at[zo, lax.rem(x + (0, 1, 3, 2)[i], NX), :, pl.ds(0, ca)]
+
+    def send_b(zo, to, way, step, i):
+        push(b_piece(zo, i), ssend.at[i], sz_b.at[way, i, step], tensor_at(to, x))
+
+    def send_a(zo, to, way, step, i):
+        push(a_piece(zo, i), ssend.at[9], sz_a.at[way, i, step], tensor_at(to, x))
 
     def send_x(zo):
         block = rows.at[zo, x, :, pl.ds(ca, wide - ca)]
@@ -119,44 +132,55 @@
 
             push(ref, ssend.at[7], sc.at[way, j], dp_at(y, 1 - c))
 
-    send_own(z, up, 0, 1)
-    send_own(z, down, 1, 1)
+    for i in range(2):
+        send_b(z, up, 0, 1, i)
+        send_b(z, down, 1, 1, i)
     for i, (xo, slot) in enumerate(((right, 0), (left, 1), (across, 2))):
         push(rows.at[z, x, :, pl.ds(0, ca)], ssend.at[2], sx_a.at[slot], tensor_at(z, xo))
     send_x(z)
-    load.wait()
+    send_a(z, up, 0, 1, 0)
+    send_a(z, down, 1, 1, 0)
+    loads[4].wait()
     for j in range(CHUNKS):
         push(wts.at[d, j], ssend.at[6], sw.at[0, j], dp_at(north, c))
         piece = (j + 2) % CHUNKS
         push(wts.at[d, piece], ssend.at[6], sw.at[1, j], dp_at(south, c))
     for j in range(CHUNKS):
         push(wts.at[d, j], ssend.at[7], sc.at[2, j], dp_at(y, 1 - c))
-    got(rows.at[z, left, :, pl.ds(0, ca)], sx_a.at[0])
-    got(rows.at[z, right, :, pl.ds(0, ca)], sx_a.at[1])
-    got(rows.at[z, across, :, pl.ds(0, ca)], sx_a.at[2])
-    send_a(z, up, 0, 1)
-    send_a(z, down, 1, 1)
+    for i, (xo, slot) in enumerate(((right, 1), (left, 0), (across, 2))):
+        got(rows.at[z, xo, :, pl.ds(0, ca)], sx_a.at[slot])
+        send_a(z, up, 0, 1, i + 1)
+        send_a(z, down, 1, 1, i + 1)
 
     def ring_step(k, _):
         below, above = lax.rem(z + nz - k, nz), lax.rem(z + k, nz)
-        got(rows.at[below, x], sz_own.at[0, k])
-        send_own(below, up, 0, k + 1)
-        got(rows.at[above, x], sz_own.at[1, k])
-
-        @pl.when(k < half - 1)
-        def _():
-            send_own(above, down, 1, k + 1)
+        for i in range(2):
+            got(b_piece(below, i), sz_b.at[0, i, k])
+
+            @pl.when((k < half - 1) | (i == 0))
+            def _():
+                send_b(below, up, 0, k + 1, i)
+
+            got(b_piece(above, i), sz_b.at[1, i, k])
+
+            @pl.when((k < half - 1) | (i == 1))
+            def _():
+                send_b(above, down, 1, k + 1, i)
 
         send_x(below)
         send_x(above)
-        got(three_a, sz_a.at[0, k])
-
-        @pl.when(k < half - 1)
-        def _():
-            send_a(below, up, 0, k + 1)
-
-        got(three_a, sz_a.at[1, k])
-        send_a(above, down, 1, k + 1)
+        for i in range(4):
+            got(a_piece(below, i), sz_a.at[0, i, k])
+
+            @pl.when((k < half - 1) | (i < 2))
+            def _():
+                send_a(below, up, 0, k + 1, i)
+
+            got(a_piece(above, i), sz_a.at[1, i, k])
+
+            @pl.when((k < half - 1) | (i >= 2))
+            def _():
+                send_a(above, down, 1, k + 1, i)
 
         forward_x(lax.rem(z + nz - k + 1, nz))
 
@@ -164,23 +188,25 @@
         def _():
             forward_x(lax.rem(z + k - 1, nz))
 
-        @pl.when(k <= EVENTS)
+        @pl.when((k > 1) & (k <= EVENTS + 1))
         def _():
-            weight_event(k - 1)
+            weight_event(k - 2)
 
         return 0
 
     lax.fori_loop(1, half, ring_step, 0)
     far = lax.rem(z + half, nz)
-    got(rows.at[far, x], sz_own.at[0, half])
+    got(b_piece(far, 0), sz_b.at[0, 0, half])
+    got(b_piece(far, 1), sz_b.at[1, 1, half])
     send_x(far)
     if half > 1:
         forward_x(lax.rem(z + half + 1, nz))
     if half > 2:
         forward_x(lax.rem(z + half - 1, nz))
-    for j in range(half - 1, EVENTS):
+    for j in range(max(half - 2, 0), EVENTS):
         weight_event(jnp.int32(j))
-    got(three_a, sz_a.at[1, half])
+    for i in range(4):
+        got(a_piece(far, i), sz_a.at[i // 2, i, half])
     forward_x(far)
 
     def last_x(zo, _):
@@ -260,26 +286,30 @@
     stats[1] = group_ent
     per = LANES // own_rows
     turn = lax.rem(LANES - t % per * own_rows, LANES)
-    for ref, s in ((logp_ref, 0), (ent_ref, 1)):
+    for s in range(2):
         line = stats[s, pl.ds(t // per, 1), :]
-        ref[...] = pltpu.roll(jnp.broadcast_to(line, (8, LANES)), turn, 1)[0:1, 0:own_rows]
+        out_ref[s:s + 1, :] = pltpu.roll(jnp.broadcast_to(line, (8, LANES)), turn, 1)[0:1, :]
 
     position = lax.broadcasted_iota(jnp.int32, shape, 0) * LANES + lax.broadcasted_iota(jnp.int32, shape, 1)
     count = lens_ref.shape[1]
-    slot = lax.broadcasted_iota(jnp.int32, (1, count), 1)
-    sums = jnp.zeros((1, count), jnp.float32)
+    slot = lax.broadcasted_iota(jnp.int32, (1, LANES), 1)
+    sums = jnp.zeros((1, LANES), jnp.float32)
+    spans = jnp.ones((1, LANES), jnp.int32)
     start = jnp.int32(0)
     for q in range(count):
         end = start + lens_ref[0, q]
         inside = (position >= start) & (position < end)
         part = jnp.sum(jnp.sum(jnp.where(inside, group_logp, 0.0), axis=0, keepdims=True), axis=1, keepdims=True)
         sums = jnp.where(slot == q, part, sums)
+        spans = jnp.where(slot == q, lens_ref[0, q], spans)
         start = end
-    mean_ref[...] = sums / lensv_ref[...].astype(jnp.float32)
-
-    got(rows.at[pl.ds(0, nz - 1), 0], ssend.at[0])
-    got(rows.at[pl.ds(0, nz - 1), pl.ds(0, 3), :, pl.ds(0, ca)], ssend.at[1])
-    got(three_a, ssend.at[2])
+    out_ref[2:3, :] = sums / spans.astype(jnp.float32)
+    out_ref[3:8, :] = jnp.zeros((5, LANES), jnp.float32)
+
+    for i in range(2):
+        got(rows.at[pl.ds(0, nz - 1), 0, :, b_cols[i]], ssend.at[i])
+    got(rows.at[pl.ds(0, nz - 1), :, :, pl.ds(0, ca)], ssend.at[9])
+    got(rows.at[0, pl.ds(0, 3), :, pl.ds(0, ca)], ssend.at[2])
     got(rows.at[:, pl.ds(0, 2), :, pl.ds(ca, wide - ca)], ssend.at[3])
     got(rows.at[:, 0, :, pl.ds(ca, cm - ca)], ssend.at[4])
     got(rows.at[:, 0, :, pl.ds(cm, wide - cm)], ssend.at[5])
@@ -296,40 +326,40 @@
     wide = width + LANES
     group_rows = nz * NX * own_rows
     vmem = pl.BlockSpec(memory_space=pltpu.VMEM)
-    smem = pl.BlockSpec(memory_space=pltpu.SMEM)
+    hbm = pl.BlockSpec(memory_space=pltpu.HBM)
     dma = pltpu.SemaphoreType.DMA
-    logp, ent, mean = pl.pallas_call(
+    out = pl.pallas_call(
         functools.partial(kernel, nz),
-        out_shape=(
-            jax.ShapeDtypeStruct((1, own_rows), jnp.float32),
-            jax.ShapeDtypeStruct((1, own_rows), jnp.float32),
-            jax.ShapeDtypeStruct(lengths.shape, jnp.float32),
-        ),
-        in_specs=[vmem, vmem, pl.BlockSpec(memory_space=pl.ANY), smem, smem, vmem],
-        out_specs=(vmem, vmem, vmem),
+        out_shape=jax.ShapeDtypeStruct((8, LANES), jnp.float32),
+        in_specs=[hbm] * 5,
+        out_specs=vmem,
         scratch_shapes=[
+            pltpu.VMEM((own_rows, width), jnp.bfloat16),
+            pltpu.VMEM((width // LANES, LANES), jnp.float32),
+            pltpu.SMEM((own_rows,), jnp.int32),
+            pltpu.SMEM(lengths.shape, jnp.int32),
             pltpu.VMEM((nz, NX, own_rows, wide), jnp.bfloat16),
             pltpu.VMEM((2 * NY, CHUNKS, depth // CHUNKS, vocab), jnp.bfloat16),
             pltpu.VMEM((256, vocab), jnp.float32),
             pltpu.VMEM((4, group_rows // LANES, LANES), jnp.float32),
             pltpu.VMEM((3, 4, 4, group_rows // LANES, LANES), jnp.float32),
-            dma((2, nz // 2 + 1)),
-            dma((2, nz // 2 + 1)),
+            dma((2, 2, nz // 2 + 1)),
+            dma((2, 4, nz // 2 + 1)),
             dma((3,)),
             dma((2, nz)),
             dma((2, nz)),
             dma((2, EVENTS)),
             dma((3, EVENTS)),
             dma((3,)),
-            dma((9,)),
-            dma,
+            dma((10,)),
+            dma((5,)),
         ],
         compiler_params=pltpu.CompilerParams(
-            collective_id=0, has_side_effects=True, vmem_limit_bytes=48 << 20
+            collective_id=0, has_side_effects=True, vmem_limit_bytes=64 << 20
         ),
-    )(hidden_states, norm_gain[None, :], head_weight.reshape(CHUNKS, depth // CHUNKS, vocab),
-      targets, lengths, lengths)
-    return logp[0], ent[0], mean
+    )(hidden_states, norm_gain.reshape(width // LANES, LANES),
+      head_weight.reshape(CHUNKS, depth // CHUNKS, vocab), targets, lengths)
+    return out[0, :own_rows], out[1, :own_rows], out[2:3, :lengths.shape[1]]
 
 
 def solution(mesh):

time: 89.3 us -> 81.7 us (0.915)
  Pallas kernels: 83.9 us -> 79.6 us
  local copies, waits for them, and re-layouts: 4.3 us -> 1.3 us
    pallas_call x1, Pallas kernels: 83.9 us -> 79.6 us  [on_device(): pl.pallas_call(functools.partial(kernel, nz), out_shape=jax.ShapeDtypeStr...]
    unnamed x11 -> x0, local copies, waits for them, and re-layouts: 3.57 us -> none
    slice x0 -> x1, local copies, waits for them, and re-layouts: none -> 1.3 us  [on_device(): return (out[0, :own_rows], out[1, :own_rows], out[2:3, :lengths.shape[1]])]
where the time goes in v2:
time: 81.7 us; the launch traced here: 81.5 us
  Pallas kernels  79.6 us (97%)
  local copies, waits for them, and re-layouts  1.3 us (2%)
    pallas_call x1, Pallas kernels, on_device(): pl.pallas_call(functools.partial(kernel, nz), out_shape=jax.ShapeDtypeStr...  79.6 us

profile of v2, /device:TPU:24, one launch (start us, length us, event | category | flops | bytes accessed | tf_op | source)
XLA Modules:
  0.0 81.5 jit_solution(1173252914537698678)
XLA Ops:
  0.6 79.6 %shard_map.76 = f32[8,128]{1,0:T(8,128)} custom-call(bf16[16,2560]{1,0:T(8,128)(2,1)} %hidden_hbm.1, f32[20,128]{1,0:T(8,128)} %bitcast.7, bf16[4,80,1188]{2,1,0:T(8,128)(2,1)} %bitcast.6, s32[16]{0:T(128)} %targets_hbm.1, s32[1,16]{1,0:T(1,128)} %lens_hbm.1), custom_call_target="tpu_custom_call" | custom-call | tf_op jit(solution)/shard_map/pallas_call | solution.py:331
  80.2 1.3 %fusion = (f32[1,16]{1,0:T(1,128)}, f32[16]{0:T(128)}, f32[16]{0:T(128)}) fusion(f32[8,128]{1,0:T(8,128)} %shard_map.76), kind=kLoop, calls=%fused_computation.2 | loop fusion | bytes 384 | tf_op jit(solution)/shard_map/slice | solution.py:362

commit v3 on v2

--- a/solution.py
+++ b/solution.py
@@ -25,7 +25,7 @@
 def kernel(nz, hidden_hbm, gain_hbm, w_hbm, targets_hbm, lens_hbm,
            out_ref,
            hidden_ref, gain_ref, targets_ref, lens_ref,
-           rows, wts, logits, stats, ex, sz_b, sz_a, sx_a, sx1, sx2, sw, sc, sex, ssend, sload):
+           rows, wts, logits, stats, ex_x, ex_z, done, sz_b, sz_a, sx_a, sx1, sx2, sw, sc, sex, ssend, sload):
     own_rows, width = hidden_ref.shape
     vocab = w_hbm.shape[-1]
     half = nz // 2
@@ -36,7 +36,6 @@
     d = lax.axis_index("dp")
     z, x = t // NX, t % NX
     y, c = d // 2, d % 2
-    zg = nz // 4
 
     def tensor_at(zz, xx):
         return {"tensor": zz * NX + xx}
@@ -109,14 +108,14 @@
 
     def send_x(zo):
         block = rows.at[zo, x, :, pl.ds(ca, wide - ca)]
-        push(block, ssend.at[3], sx1.at[0, zo], tensor_at(z, right))
-        push(block, ssend.at[3], sx1.at[1, zo], tensor_at(z, left))
+        push(block, ssend.at[8], sx1.at[0, zo], tensor_at(z, right))
+        push(block, ssend.at[8], sx1.at[1, zo], tensor_at(z, left))
 
     def forward_x(zo):
         got(rows.at[zo, left, :, pl.ds(ca, wide - ca)], sx1.at[0, zo])
-        push(rows.at[zo, left, :, pl.ds(ca, cm - ca)], ssend.at[4], sx2.at[0, zo], tensor_at(z, right))
+        push(rows.at[zo, left, :, pl.ds(ca, cm - ca)], ssend.at[10], sx2.at[0, zo], tensor_at(z, right))
         got(rows.at[zo, right, :, pl.ds(ca, wide - ca)], sx1.at[1, zo])
-        push(rows.at[zo, right, :, pl.ds(cm, wide - cm)], ssend.at[5], sx2.at[1, zo], tensor_at(z, left))
+        push(rows.at[zo, right, :, pl.ds(cm, wide - cm)], ssend.at[11], sx2.at[1, zo], tensor_at(z, left))
 
     def weight_event(j):
         for way in (0, 1):
@@ -205,16 +204,6 @@
         forward_x(lax.rem(z + half - 1, nz))
     for j in range(max(half - 2, 0), EVENTS):
         weight_event(jnp.int32(j))
-    for i in range(4):
-        got(a_piece(far, i), sz_a.at[i // 2, i, half])
-    forward_x(far)
-
-    def last_x(zo, _):
-        got(rows.at[zo, across, :, pl.ds(ca, cm - ca)], sx2.at[0, zo])
-        got(rows.at[zo, across, :, pl.ds(cm, wide - cm)], sx2.at[1, zo])
-        return 0
-
-    lax.fori_loop(0, nz, last_x, 0)
 
     def last_w(j, _):
         got(wts.at[0, 0], sc.at[0, j])
@@ -225,18 +214,30 @@
     for j in range(CHUNKS):
         got(wts.at[0, 0], sc.at[2, j])
 
-    zs = 256 // (NX * own_rows)
-    block = 256
+    pairs = nz // 2
+    pair_rows = 2 * NX * own_rows
     vocab_start = t * vocab
     lane_w = lax.broadcasted_iota(jnp.int32, (1, LANES), 1)
     digit_weights = jnp.where(lane_w == 0, 65536.0, jnp.where(lane_w == 1, 256.0, jnp.where(lane_w == 2, 1.0, 0.0)))
 
-    def score(b, _):
-        held = rows.at[pl.ds(b * zs, zs)]
-        lhs = held[:, :, :, 0:width].reshape(block, width)
+    def score(j, _):
+        @pl.when(j == 1)
+        def _():
+            for i in range(4):
+                got(a_piece(far, i), sz_a.at[i // 2, i, half])
+            forward_x(far)
+
+        both = (lax.rem(z // 2 + pairs - j, pairs), lax.rem(z // 2 + 1 + j, pairs))
+        for pair in both:
+            for i in range(2):
+                zo = pair * 2 + i
+                got(rows.at[zo, across, :, b_cols[0]], sx2.at[0, zo])
+                got(rows.at[zo, across, :, b_cols[1]], sx2.at[1, zo])
+        held = [rows[pl.ds(pair * 2, 2)].reshape(pair_rows, wide) for pair in both]
+        held = jnp.concatenate(held, axis=0)
         rhs = wts[...].reshape(width, vocab)
-        logits[...] = jnp.dot(lhs, rhs, preferred_element_type=jnp.float32)
-        coded = held[:, :, :, width:wide].reshape(block, LANES).astype(jnp.float32)
+        logits[...] = jnp.dot(held[:, 0:width], rhs, preferred_element_type=jnp.float32)
+        coded = held[:, width:wide].astype(jnp.float32)
         wanted = jnp.sum(coded * digit_weights, axis=1, keepdims=True).astype(jnp.int32) - vocab_start
         values = logits[...]
         highest = jnp.max(values, axis=1, keepdims=True)
@@ -245,49 +246,55 @@
         weighted = jnp.sum(expo * values, axis=1, keepdims=True)
         columns = lax.broadcasted_iota(jnp.int32, values.shape, 1)
         picked = jnp.sum(jnp.where(columns == wanted, values, 0.0), axis=1, keepdims=True)
-        at = lax.broadcasted_iota(jnp.int32, (block, LANES), 1)
+        at = lax.broadcasted_iota(jnp.int32, (2 * pair_rows, LANES), 1)
         table = jnp.where(at == 0, highest, jnp.where(at == 1, total, jnp.where(at == 2, weighted, picked)))
         flat = jnp.transpose(table)
-        for s in range(4):
-            for q in range(block // LANES):
-                stats[s, pl.ds(b * (block // LANES) + q, 1), :] = flat[s:s + 1, q * LANES:(q + 1) * LANES]
+        for i, pair in enumerate(both):
+            for s in range(4):
+                stats[pair // 2, pl.ds(2 * s + pair % 2, 1), :] = flat[s:s + 1, i * LANES:(i + 1) * LANES]
         return 0
 
-    lax.fori_loop(0, nz // zs, score, 0)
-
-    def exchange(stage, mine, size, peer_of):
-        ex[stage, mine] = stats[...]
-        for i in range(1, size):
-            push(ex.at[stage, mine], ssend.at[8], sex.at[stage], peer_of(lax.rem(mine + i, size)))
-        if size > 1:
-            got(ex.at[stage, pl.ds(0, size - 1)], sex.at[stage])
-        top = ex[stage, 0, 0]
-        for i in range(1, size):
-            top = jnp.maximum(top, ex[stage, i, 0])
+    lax.fori_loop(0, pairs // 2, score, 0)
+
+    def combine(held):
+        top = held[0][0:2]
+        for one in held[1:]:
+            top = jnp.maximum(top, one[0:2])
         sums = [jnp.zeros_like(top) for _ in range(3)]
-        for i in range(size):
-            factor = jnp.exp(ex[stage, i, 0] - top)
-            sums[0] += ex[stage, i, 1] * factor
-            sums[1] += ex[stage, i, 2] * factor
-            sums[2] += ex[stage, i, 3]
-        stats[0] = top
-        for i in range(3):
-            stats[i + 1] = sums[i]
-
-    exchange(0, x, NX, lambda i: tensor_at(z, i))
-    exchange(1, z % 4, 4, lambda i: tensor_at(z // 4 * 4 + i, x))
-    exchange(2, z // 4, zg, lambda i: tensor_at(i * 4 + z % 4, x))
-
-    lse = stats[0] + jnp.log(stats[1])
-    group_logp = stats[3] - lse
-    group_ent = lse - stats[2] / stats[1]
+        for one in held:
+            factor = jnp.exp(one[0:2] - top)
+            sums[0] += one[2:4] * factor
+            sums[1] += one[4:6] * factor
+            sums[2] += one[6:8]
+        return top, sums
+
+    quarters = pairs // 2
+    ex_x[x] = stats[x]
+    for i in (1, 2, 3):
+        xo = lax.rem(x + i, NX)
+        pltpu.make_async_remote_copy(
+            src_ref=stats.at[xo], dst_ref=ex_x.at[x], send_sem=ssend.at[3], recv_sem=sex.at[0],
+            device_id=tensor_at(z, xo), device_id_type=MESH,
+        ).start()
+    got(ex_x.at[pl.ds(0, NX - 1)], sex.at[0])
+    top, sums = combine([ex_x[i] for i in range(NX)])
+    ex_z[z] = jnp.concatenate([top] + sums, axis=0)
+    for i in range(1, nz):
+        push(ex_z.at[z], ssend.at[4], sex.at[1], tensor_at(lax.rem(z + i, nz), x))
+    got(ex_z.at[pl.ds(0, nz - 1)], sex.at[1])
+    top, sums = combine([ex_z[i] for i in range(nz)])
+    lse = top + jnp.log(sums[0])
+    done[x, 0:2, :] = sums[2] - lse
+    done[x, 2:4, :] = lse - sums[1] / sums[0]
+    for i in (1, 2, 3):
+        push(done.at[x], ssend.at[5], sex.at[2], tensor_at(z, lax.rem(x + i, NX)))
+    got(done.at[pl.ds(0, NX - 1)], sex.at[2])
+    group_logp = jnp.concatenate([done[i, 0:2] for i in range(quarters)], axis=0)
     shape = group_logp.shape
-    stats[0] = group_logp
-    stats[1] = group_ent
     per = LANES // own_rows
     turn = lax.rem(LANES - t % per * own_rows, LANES)
     for s in range(2):
-        line = stats[s, pl.ds(t // per, 1), :]
+        line = done[t // per // 2, pl.ds(2 * s + t // per % 2, 1), :]
         out_ref[s:s + 1, :] = pltpu.roll(jnp.broadcast_to(line, (8, LANES)), turn, 1)[0:1, :]
 
     position = lax.broadcasted_iota(jnp.int32, shape, 0) * LANES + lax.broadcasted_iota(jnp.int32, shape, 1)
@@ -310,14 +317,14 @@
         got(rows.at[pl.ds(0, nz - 1), 0, :, b_cols[i]], ssend.at[i])
     got(rows.at[pl.ds(0, nz - 1), :, :, pl.ds(0, ca)], ssend.at[9])
     got(rows.at[0, pl.ds(0, 3), :, pl.ds(0, ca)], ssend.at[2])
-    got(rows.at[:, pl.ds(0, 2), :, pl.ds(ca, wide - ca)], ssend.at[3])
-    got(rows.at[:, 0, :, pl.ds(ca, cm - ca)], ssend.at[4])
-    got(rows.at[:, 0, :, pl.ds(cm, wide - cm)], ssend.at[5])
+    got(rows.at[:, pl.ds(0, 2), :, pl.ds(ca, wide - ca)], ssend.at[8])
+    got(rows.at[:, 0, :, b_cols[0]], ssend.at[10])
+    got(rows.at[:, 0, :, b_cols[1]], ssend.at[11])
     got(wts.at[pl.ds(0, 3)], ssend.at[6])
     got(wts.at[pl.ds(0, 4)], ssend.at[7])
-    for stage, size in ((0, NX), (1, 4), (2, zg)):
-        if size > 1:
-            got(ex.at[stage, pl.ds(0, size - 1)], ssend.at[8])
+    got(ex_x.at[pl.ds(0, NX - 1)], ssend.at[3])
+    got(ex_z.at[pl.ds(0, nz - 1)], ssend.at[4])
+    got(done.at[pl.ds(0, NX - 1)], ssend.at[5])
 
 
 def on_device(nz, hidden_states, norm_gain, head_weight, targets, lengths):
@@ -341,8 +348,10 @@
             pltpu.VMEM((nz, NX, own_rows, wide), jnp.bfloat16),
             pltpu.VMEM((2 * NY, CHUNKS, depth // CHUNKS, vocab), jnp.bfloat16),
             pltpu.VMEM((256, vocab), jnp.float32),
-            pltpu.VMEM((4, group_rows // LANES, LANES), jnp.float32),
-            pltpu.VMEM((3, 4, 4, group_rows // LANES, LANES), jnp.float32),
+            pltpu.VMEM((group_rows // LANES // 2, 8, LANES), jnp.float32),
+            pltpu.VMEM((NX, 8, LANES), jnp.float32),
+            pltpu.VMEM((nz, 8, LANES), jnp.float32),
+            pltpu.VMEM((NX, 4, LANES), jnp.float32),
             dma((2, 2, nz // 2 + 1)),
             dma((2, 4, nz // 2 + 1)),
             dma((3,)),
@@ -351,7 +360,7 @@
             dma((2, EVENTS)),
             dma((3, EVENTS)),
             dma((3,)),
-            dma((10,)),
+            dma((12,)),
             dma((5,)),
         ],
         compiler_params=pltpu.CompilerParams(

time: 81.7 us -> 75 us (0.918)
  Pallas kernels: 79.6 us -> 72.8 us
    pallas_call x1, Pallas kernels: 79.6 us -> 72.8 us  [on_device(): pl.pallas_call(functools.partial(kernel, nz), out_shape=jax.ShapeDtypeStr...]
where the time goes in v3:
time: 75 us; the launch traced here: 74.8 us
  Pallas kernels  72.8 us (97%)
  local copies, waits for them, and re-layouts  1.3 us (2%)
    pallas_call x1, Pallas kernels, on_device(): pl.pallas_call(functools.partial(kernel, nz), out_shape=jax.ShapeDtypeStr...  72.8 us

profile of v3, /device:TPU:24, one launch (start us, length us, event | category | flops | bytes accessed | tf_op | source)
XLA Modules:
  0.0 74.8 jit_solution(1841916634274028203)
XLA Ops:
  0.6 72.8 %shard_map.76 = f32[8,128]{1,0:T(8,128)} custom-call(bf16[16,2560]{1,0:T(8,128)(2,1)} %hidden_hbm.1, f32[20,128]{1,0:T(8,128)} %bitcast.7, bf16[4,80,1188]{2,1,0:T(8,128)(2,1)} %bitcast.6, s32[16]{0:T(128)} %targets_hbm.1, s32[1,16]{1,0:T(1,128)} %lens_hbm.1), custom_call_target="tpu_custom_call" | custom-call | tf_op jit(solution)/shard_map/pallas_call | solution.py:338
  73.5 1.3 %fusion = (f32[1,16]{1,0:T(1,128)}, f32[16]{0:T(128)}, f32[16]{0:T(128)}) fusion(f32[8,128]{1,0:T(8,128)} %shard_map.76), kind=kLoop, calls=%fused_computation.2 | loop fusion | bytes 384 | tf_op jit(solution)/shard_map/slice | solution.py:371

commit v4 on v3

--- a/solution.py
+++ b/solution.py
@@ -111,6 +111,14 @@
         push(block, ssend.at[8], sx1.at[0, zo], tensor_at(z, right))
         push(block, ssend.at[8], sx1.at[1, zo], tensor_at(z, left))
 
+    def send_across(zo):
+        for i in range(2):
+            push(b_piece(zo, i), ssend.at[10 + i], sx2.at[i, zo], tensor_at(z, across))
+
+    def got_sides(zo):
+        got(rows.at[zo, left, :, pl.ds(ca, wide - ca)], sx1.at[0, zo])
+        got(rows.at[zo, right, :, pl.ds(ca, wide - ca)], sx1.at[1, zo])
+
     def forward_x(zo):
         got(rows.at[zo, left, :, pl.ds(ca, wide - ca)], sx1.at[0, zo])
         push(rows.at[zo, left, :, pl.ds(ca, cm - ca)], ssend.at[10], sx2.at[0, zo], tensor_at(z, right))
@@ -134,16 +142,16 @@
     for i in range(2):
         send_b(z, up, 0, 1, i)
         send_b(z, down, 1, 1, i)
+    loads[4].wait()
+    for j in range(CHUNKS):
+        push(wts.at[d, j], ssend.at[6], sw.at[0, j], dp_at(north, c))
+        piece = (j + 2) % CHUNKS
+        push(wts.at[d, piece], ssend.at[6], sw.at[1, j], dp_at(south, c))
     for i, (xo, slot) in enumerate(((right, 0), (left, 1), (across, 2))):
         push(rows.at[z, x, :, pl.ds(0, ca)], ssend.at[2], sx_a.at[slot], tensor_at(z, xo))
     send_x(z)
     send_a(z, up, 0, 1, 0)
     send_a(z, down, 1, 1, 0)
-    loads[4].wait()
-    for j in range(CHUNKS):
-        push(wts.at[d, j], ssend.at[6], sw.at[0, j], dp_at(north, c))
-        piece = (j + 2) % CHUNKS
-        push(wts.at[d, piece], ssend.at[6], sw.at[1, j], dp_at(south, c))
     for j in range(CHUNKS):
         push(wts.at[d, j], ssend.at[7], sc.at[2, j], dp_at(y, 1 - c))
     for i, (xo, slot) in enumerate(((right, 1), (left, 0), (across, 2))):
@@ -168,6 +176,12 @@
 
         send_x(below)
         send_x(above)
+
+        @pl.when(k == half - 1)
+        def _():
+            send_across(below)
+            send_across(above)
+
         for i in range(4):
             got(a_piece(below, i), sz_a.at[0, i, k])
 
@@ -187,9 +201,9 @@
         def _():
             forward_x(lax.rem(z + k - 1, nz))
 
-        @pl.when((k > 1) & (k <= EVENTS + 1))
+        @pl.when(k <= EVENTS)
         def _():
-            weight_event(k - 2)
+            weight_event(k - 1)
 
         return 0
 
@@ -198,11 +212,8 @@
     got(b_piece(far, 0), sz_b.at[0, 0, half])
     got(b_piece(far, 1), sz_b.at[1, 1, half])
     send_x(far)
-    if half > 1:
-        forward_x(lax.rem(z + half + 1, nz))
-    if half > 2:
-        forward_x(lax.rem(z + half - 1, nz))
-    for j in range(max(half - 2, 0), EVENTS):
+    send_across(far)
+    for j in range(half - 1, EVENTS):
         weight_event(jnp.int32(j))
 
     def last_w(j, _):
@@ -220,24 +231,34 @@
     lane_w = lax.broadcasted_iota(jnp.int32, (1, LANES), 1)
     digit_weights = jnp.where(lane_w == 0, 65536.0, jnp.where(lane_w == 1, 256.0, jnp.where(lane_w == 2, 1.0, 0.0)))
 
-    def score(j, _):
-        @pl.when(j == 1)
-        def _():
+    def pairs_of(j):
+        return lax.rem(z // 2 + pairs - j, pairs), lax.rem(z // 2 + 1 + j, pairs)
+
+    def arrived(j):
+        if j == pairs // 2 - 2:
+            got_sides(lax.rem(z + nz - half + 1, nz))
+            got_sides(lax.rem(z + half - 1, nz))
+        if j == pairs // 2 - 1:
             for i in range(4):
                 got(a_piece(far, i), sz_a.at[i // 2, i, half])
-            forward_x(far)
-
-        both = (lax.rem(z // 2 + pairs - j, pairs), lax.rem(z // 2 + 1 + j, pairs))
-        for pair in both:
+            got_sides(far)
+        for pair in pairs_of(j):
             for i in range(2):
                 zo = pair * 2 + i
                 got(rows.at[zo, across, :, b_cols[0]], sx2.at[0, zo])
                 got(rows.at[zo, across, :, b_cols[1]], sx2.at[1, zo])
-        held = [rows[pl.ds(pair * 2, 2)].reshape(pair_rows, wide) for pair in both]
+
+    def multiply(j):
+        held = [rows[pl.ds(pair * 2, 2)].reshape(pair_rows, wide) for pair in pairs_of(j)]
         held = jnp.concatenate(held, axis=0)
         rhs = wts[...].reshape(width, vocab)
         logits[...] = jnp.dot(held[:, 0:width], rhs, preferred_element_type=jnp.float32)
-        coded = held[:, width:wide].astype(jnp.float32)
+
+    def summarize(j):
+        both = pairs_of(j)
+        coded = jnp.concatenate(
+            [rows[pl.ds(pair * 2, 2), :, :, width:wide].reshape(pair_rows, LANES) for pair in both], axis=0
+        ).astype(jnp.float32)
         wanted = jnp.sum(coded * digit_weights, axis=1, keepdims=True).astype(jnp.int32) - vocab_start
         values = logits[...]
         highest = jnp.max(values, axis=1, keepdims=True)
@@ -252,6 +273,15 @@
         for i, pair in enumerate(both):
             for s in range(4):
                 stats[pair // 2, pl.ds(2 * s + pair % 2, 1), :] = flat[s:s + 1, i * LANES:(i + 1) * LANES]
+
+    def score(j, _):
+        for jj in range(pairs // 2):
+            @pl.when(j == jj)
+            def _():
+                arrived(jj)
+
+        multiply(j)
+        summarize(j)
         return 0
 
     lax.fori_loop(0, pairs // 2, score, 0)
@@ -278,14 +308,17 @@
         ).start()
     got(ex_x.at[pl.ds(0, NX - 1)], sex.at[0])
     top, sums = combine([ex_x[i] for i in range(NX)])
-    ex_z[z] = jnp.concatenate([top] + sums, axis=0)
+    ex_z[z] = jnp.concatenate([top + jnp.log(sums[0]), sums[1] / sums[0], sums[2]], axis=0)
     for i in range(1, nz):
         push(ex_z.at[z], ssend.at[4], sex.at[1], tensor_at(lax.rem(z + i, nz), x))
     got(ex_z.at[pl.ds(0, nz - 1)], sex.at[1])
-    top, sums = combine([ex_z[i] for i in range(nz)])
-    lse = top + jnp.log(sums[0])
-    done[x, 0:2, :] = sums[2] - lse
-    done[x, 2:4, :] = lse - sums[1] / sums[0]
+    held = [ex_z[i] for i in range(nz)]
+    top = functools.reduce(jnp.maximum, [one[0:2] for one in held])
+    shares = [jnp.exp(one[0:2] - top) for one in held]
+    total = sum(shares)
+    lse = top + jnp.log(total)
+    done[x, 0:2, :] = sum(one[4:6] for one in held) - lse
+    done[x, 2:4, :] = lse - sum(share * one[2:4] for share, one in zip(shares, held)) / total
     for i in (1, 2, 3):
         push(done.at[x], ssend.at[5], sex.at[2], tensor_at(z, lax.rem(x + i, NX)))
     got(done.at[pl.ds(0, NX - 1)], sex.at[2])
@@ -350,7 +383,7 @@
             pltpu.VMEM((256, vocab), jnp.float32),
             pltpu.VMEM((group_rows // LANES // 2, 8, LANES), jnp.float32),
             pltpu.VMEM((NX, 8, LANES), jnp.float32),
-            pltpu.VMEM((nz, 8, LANES), jnp.float32),
+            pltpu.VMEM((nz, 6, LANES), jnp.float32),
             pltpu.VMEM((NX, 4, LANES), jnp.float32),
             dma((2, 2, nz // 2 + 1)),
             dma((2, 4, nz // 2 + 1)),

time: 75 us -> 73.3 us (0.977)
  Pallas kernels: 72.8 us -> 70.6 us
    pallas_call x1, Pallas kernels: 72.8 us -> 70.6 us  [on_device(): pl.pallas_call(functools.partial(kernel, nz), out_shape=jax.ShapeDtypeStr...]
where the time goes in v4:
time: 73.3 us; the launch traced here: 72.6 us
  Pallas kernels  70.6 us (96%)
  local copies, waits for them, and re-layouts  1.3 us (2%)
    pallas_call x1, Pallas kernels, on_device(): pl.pallas_call(functools.partial(kernel, nz), out_shape=jax.ShapeDtypeStr...  70.6 us

profile of v4, /device:TPU:24, one launch (start us, length us, event | category | flops | bytes accessed | tf_op | source)
XLA Modules:
  0.0 72.6 jit_solution(17727208112376901008)
XLA Ops:
  0.6 70.6 %shard_map.76 = f32[8,128]{1,0:T(8,128)} custom-call(bf16[16,2560]{1,0:T(8,128)(2,1)} %hidden_hbm.1, f32[20,128]{1,0:T(8,128)} %bitcast.7, bf16[4,80,1188]{2,1,0:T(8,128)(2,1)} %bitcast.6, s32[16]{0:T(128)} %targets_hbm.1, s32[1,16]{1,0:T(1,128)} %lens_hbm.1), custom_call_target="tpu_custom_call" | custom-call | tf_op jit(solution)/shard_map/pallas_call | solution.py:371
  71.3 1.3 %fusion = (f32[1,16]{1,0:T(1,128)}, f32[16]{0:T(128)}, f32[16]{0:T(128)}) fusion(f32[8,128]{1,0:T(8,128)} %shard_map.76), kind=kLoop, calls=%fused_computation.2 | loop fusion | bytes 384 | tf_op jit(solution)/shard_map/slice | solution.py:404

commit v5 on v4

--- a/solution.py
+++ b/solution.py
@@ -18,19 +18,19 @@
 def split_columns(width):
     tiles = width // LANES
     first = max(1, round(tiles * 0.4)) * LANES
-    rest = (width - first) // LANES + 1
+    rest = (width - first) // LANES
     return first, first + rest // 2 * LANES
 
 
 def kernel(nz, hidden_hbm, gain_hbm, w_hbm, targets_hbm, lens_hbm,
            out_ref,
            hidden_ref, gain_ref, targets_ref, lens_ref,
-           rows, wts, logits, stats, ex_x, ex_z, done, sz_b, sz_a, sx_a, sx1, sx2, sw, sc, sex, ssend, sload):
+           rows, ids, wts, logits, stats, ex_x, ex_z, done, si_x, si_z, sz_b, sz_a, sx_a, sx1, sx2, sw, sc, sex, ssend, sload):
     own_rows, width = hidden_ref.shape
     vocab = w_hbm.shape[-1]
     half = nz // 2
     ca, cm = split_columns(width)
-    wide = width + LANES
+    wide = width
 
     t = lax.axis_index("tensor")
     d = lax.axis_index("dp")
@@ -72,14 +72,11 @@
     for i in range(width // LANES):
         cols = slice(i * LANES, (i + 1) * LANES)
         rows[z, x, :, cols] = (scaled[:, cols] * gain_ref[i:i + 1, :]).astype(jnp.bfloat16)
-    row_id = lax.broadcasted_iota(jnp.int32, (own_rows, LANES), 0)
-    lane = lax.broadcasted_iota(jnp.int32, (own_rows, LANES), 1)
-    ids = jnp.zeros((own_rows, LANES), jnp.int32)
+    lane = lax.broadcasted_iota(jnp.int32, (1, LANES), 1)
+    own_ids = jnp.zeros((1, LANES), jnp.int32)
     for i in range(own_rows):
-        ids = jnp.where(row_id == i, targets_ref[i], ids)
-    digits = jnp.where(lane == 0, ids >> 16, jnp.where(lane == 1, (ids >> 8) & 255, ids & 255))
-    digits = jnp.where(lane < 3, digits, 0)
-    rows[z, x, :, width:wide] = digits.astype(jnp.float32).astype(jnp.bfloat16)
+        own_ids = jnp.where(lane == i, targets_ref[i], own_ids)
+    ids[z, x] = own_ids.astype(jnp.float32)
 
     pl.semaphore_wait(barrier, len(peers))
 
@@ -149,6 +146,7 @@
         push(wts.at[d, piece], ssend.at[6], sw.at[1, j], dp_at(south, c))
     for i, (xo, slot) in enumerate(((right, 0), (left, 1), (across, 2))):
         push(rows.at[z, x, :, pl.ds(0, ca)], ssend.at[2], sx_a.at[slot], tensor_at(z, xo))
+        push(ids.at[z, x], ssend.at[12], si_x.at[slot], tensor_at(z, xo))
     send_x(z)
     send_a(z, up, 0, 1, 0)
     send_a(z, down, 1, 1, 0)
@@ -158,6 +156,10 @@
         got(rows.at[z, xo, :, pl.ds(0, ca)], sx_a.at[slot])
         send_a(z, up, 0, 1, i + 1)
         send_a(z, down, 1, 1, i + 1)
+    for xo, slot in ((right, 1), (left, 0), (across, 2)):
+        got(ids.at[z, xo], si_x.at[slot])
+    push(ids.at[z], ssend.at[13], si_z.at[0, 1], tensor_at(up, x))
+    push(ids.at[z], ssend.at[13], si_z.at[1, 1], tensor_at(down, x))
 
     def ring_step(k, _):
         below, above = lax.rem(z + nz - k, nz), lax.rem(z + k, nz)
@@ -194,6 +196,14 @@
             @pl.when((k < half - 1) | (i >= 2))
             def _():
                 send_a(above, down, 1, k + 1, i)
+
+        got(ids.at[below], si_z.at[0, k])
+        push(ids.at[below], ssend.at[13], si_z.at[0, k + 1], tensor_at(up, x))
+        got(ids.at[above], si_z.at[1, k])
+
+        @pl.when(k < half - 1)
+        def _():
+            push(ids.at[above], ssend.at[13], si_z.at[1, k + 1], tensor_at(down, x))
 
         forward_x(lax.rem(z + nz - k + 1, nz))
 
@@ -228,9 +238,6 @@
     pairs = nz // 2
     pair_rows = 2 * NX * own_rows
     vocab_start = t * vocab
-    lane_w = lax.broadcasted_iota(jnp.int32, (1, LANES), 1)
-    digit_weights = jnp.where(lane_w == 0, 65536.0, jnp.where(lane_w == 1, 256.0, jnp.where(lane_w == 2, 1.0, 0.0)))
-
     def pairs_of(j):
         return lax.rem(z // 2 + pairs - j, pairs), lax.rem(z // 2 + 1 + j, pairs)
 
@@ -242,6 +249,7 @@
             for i in range(4):
                 got(a_piece(far, i), sz_a.at[i // 2, i, half])
             got_sides(far)
+            got(ids.at[far], si_z.at[0, half])
         for pair in pairs_of(j):
             for i in range(2):
                 zo = pair * 2 + i
@@ -256,10 +264,12 @@
 
     def summarize(j):
         both = pairs_of(j)
-        coded = jnp.concatenate(
-            [rows[pl.ds(pair * 2, 2), :, :, width:wide].reshape(pair_rows, LANES) for pair in both], axis=0
-        ).astype(jnp.float32)
-        wanted = jnp.sum(coded * digit_weights, axis=1, keepdims=True).astype(jnp.int32) - vocab_start
+        spread = jnp.concatenate(
+            [jnp.broadcast_to(ids[pl.ds(pair * 2, 2)], (2, NX, own_rows, LANES)).reshape(pair_rows, LANES)
+             for pair in both], axis=0)
+        row = lax.rem(lax.broadcasted_iota(jnp.int32, spread.shape, 0), own_rows)
+        own_lane = lax.broadcasted_iota(jnp.int32, spread.shape, 1) == row
+        wanted = jnp.sum(jnp.where(own_lane, spread, 0.0), axis=1, keepdims=True).astype(jnp.int32) - vocab_start
         values = logits[...]
         highest = jnp.max(values, axis=1, keepdims=True)
         expo = jnp.exp(values - highest)
@@ -300,7 +310,7 @@
 
     quarters = pairs // 2
     ex_x[x] = stats[x]
-    for i in (1, 2, 3):
+    for i in (2, 1, 3):
         xo = lax.rem(x + i, NX)
         pltpu.make_async_remote_copy(
             src_ref=stats.at[xo], dst_ref=ex_x.at[x], send_sem=ssend.at[3], recv_sem=sex.at[0],
@@ -309,7 +319,7 @@
     got(ex_x.at[pl.ds(0, NX - 1)], sex.at[0])
     top, sums = combine([ex_x[i] for i in range(NX)])
     ex_z[z] = jnp.concatenate([top + jnp.log(sums[0]), sums[1] / sums[0], sums[2]], axis=0)
-    for i in range(1, nz):
+    for i in sorted(range(1, nz), key=lambda i: -min(i, nz - i)):
         push(ex_z.at[z], ssend.at[4], sex.at[1], tensor_at(lax.rem(z + i, nz), x))
     got(ex_z.at[pl.ds(0, nz - 1)], sex.at[1])
     held = [ex_z[i] for i in range(nz)]
@@ -319,7 +329,7 @@
     lse = top + jnp.log(total)
     done[x, 0:2, :] = sum(one[4:6] for one in held) - lse
     done[x, 2:4, :] = lse - sum(share * one[2:4] for share, one in zip(shares, held)) / total
-    for i in (1, 2, 3):
+    for i in (2, 1, 3):
         push(done.at[x], ssend.at[5], sex.at[2], tensor_at(z, lax.rem(x + i, NX)))
     got(done.at[pl.ds(0, NX - 1)], sex.at[2])
     group_logp = jnp.concatenate([done[i, 0:2] for i in range(quarters)], axis=0)
@@ -355,6 +365,8 @@
     got(rows.at[:, 0, :, b_cols[1]], ssend.at[11])
     got(wts.at[pl.ds(0, 3)], ssend.at[6])
     got(wts.at[pl.ds(0, 4)], ssend.at[7])
+    got(ids.at[0, pl.ds(0, 3)], ssend.at[12])
+    got(ids.at[pl.ds(0, nz - 1)], ssend.at[13])
     got(ex_x.at[pl.ds(0, NX - 1)], ssend.at[3])
     got(ex_z.at[pl.ds(0, nz - 1)], ssend.at[4])
     got(done.at[pl.ds(0, NX - 1)], ssend.at[5])
@@ -363,7 +375,6 @@
 def on_device(nz, hidden_states, norm_gain, head_weight, targets, lengths):
     own_rows, width = hidden_states.shape
     depth, vocab = head_weight.shape
-    wide = width + LANES
     group_rows = nz * NX * own_rows
     vmem = pl.BlockSpec(memory_space=pltpu.VMEM)
     hbm = pl.BlockSpec(memory_space=pltpu.HBM)
@@ -378,13 +389,16 @@
             pltpu.VMEM((width // LANES, LANES), jnp.float32),
             pltpu.SMEM((own_rows,), jnp.int32),
             pltpu.SMEM(lengths.shape, jnp.int32),
-            pltpu.VMEM((nz, NX, own_rows, wide), jnp.bfloat16),
+            pltpu.VMEM((nz, NX, own_rows, width), jnp.bfloat16),
+            pltpu.VMEM((nz, NX, 1, LANES), jnp.float32),
             pltpu.VMEM((2 * NY, CHUNKS, depth // CHUNKS, vocab), jnp.bfloat16),
             pltpu.VMEM((256, vocab), jnp.float32),
             pltpu.VMEM((group_rows // LANES // 2, 8, LANES), jnp.float32),
             pltpu.VMEM((NX, 8, LANES), jnp.float32),
             pltpu.VMEM((nz, 6, LANES), jnp.float32),
             pltpu.VMEM((NX, 4, LANES), jnp.float32),
+            dma((3,)),
+            dma((2, nz // 2 + 1)),
             dma((2, 2, nz // 2 + 1)),
             dma((2, 4, nz // 2 + 1)),
             dma((3,)),
@@ -393,7 +407,7 @@
             dma((2, EVENTS)),
             dma((3, EVENTS)),
             dma((3,)),
-            dma((12,)),
+            dma((14,)),
             dma((5,)),
         ],
         compiler_params=pltpu.CompilerParams(

time: 73.3 us -> 72.6 us (level)
  no operation moved by 1% of the time
where the time goes in v5:
time: 72.6 us; the launch traced here: 71.9 us
  Pallas kernels  69.9 us (96%)
  local copies, waits for them, and re-layouts  1.3 us (2%)
    pallas_call x1, Pallas kernels, on_device(): pl.pallas_call(functools.partial(kernel, nz), out_shape=jax.ShapeDtypeStr...  69.9 us

profile of v5, /device:TPU:24, one launch (start us, length us, event | category | flops | bytes accessed | tf_op | source)
XLA Modules:
  0.0 71.9 jit_solution(8318737156468515836)
XLA Ops:
  0.6 69.9 %shard_map.76 = f32[8,128]{1,0:T(8,128)} custom-call(bf16[16,2560]{1,0:T(8,128)(2,1)} %hidden_hbm.1, f32[20,128]{1,0:T(8,128)} %bitcast.7, bf16[4,80,1188]{2,1,0:T(8,128)(2,1)} %bitcast.6, s32[16]{0:T(128)} %targets_hbm.1, s32[1,16]{1,0:T(1,128)} %lens_hbm.1), custom_call_target="tpu_custom_call" | custom-call | tf_op jit(solution)/shard_map/pallas_call | solution.py:382
  70.6 1.3 %fusion = (f32[1,16]{1,0:T(1,128)}, f32[16]{0:T(128)}, f32[16]{0:T(128)}) fusion(f32[8,128]{1,0:T(8,128)} %shard_map.76), kind=kLoop, calls=%fused_computation.2 | loop fusion | bytes 384 | tf_op jit(solution)/shard_map/slice | solution.py:418
